TPU v7x, 128 devices: a whole 4x4x4 slice. The times are simulated.
128 devices in a mesh: leaf: 16 (over y_hi, x, core), rep: 8 (over y_lo, z).
Axes of the slice: x: 4, y: 4 (y_hi: 2, y_lo: 2; y = y_hi * 2 + y_lo), z: 4, core: 2. Of those that a mesh axis runs over, the one named last changes fastest.
Arguments:
- local_right: float32 [16, 8, 2048, 128], P('leaf', 'rep'), may hold values from -6 to 6
- local_inverse: bfloat16 [16, 8, 16, 128, 128], P('leaf', 'rep'), may hold values from -1 to 1.4, as said below
- local_below: bfloat16 [16, 8, 15, 128, 128], P('leaf', 'rep'), may hold values from -0.5 to 0.5
- local_parent: int32 [16, 8, 15], P('leaf', 'rep'), may hold values from 1 to 15, as said below
- local_coupling: bfloat16 [16, 8, 4, 384, 2048], P('leaf', 'rep'), may hold values from -0.1 to 0.1
- separator_right: float32 [15, 384, 128], replicated, may hold values from -6 to 6
- separator_inverse: bfloat16 [15, 3, 128, 128], replicated, may hold values from -1 to 1.4, as said below
- separator_lower: bfloat16 [15, 384, 384], replicated, may hold values from -0.3125 to 0.3125
- parent_coupling: bfloat16 [14, 384, 384], replicated, may hold values from -0.3125 to 0.3125
Outputs:
- local_solution: float32 [16, 8, 2048, 128], P('leaf', 'rep')
- separator_solution: float32 [16, 4, 384, 128], P('leaf')
Inputs may be any that keep to these rules, and one draw needn't show every extreme that they name: `local_parent`: entry k of a device's list is larger than k. `local_inverse`: every block is lower triangular. `separator_inverse`: every block is lower triangular.
All inputs are finite; a program needn't handle non-finite values.
Results may differ from a plain program's by a relative error of at most 0.035.
Values sent between devices are 32-bit elements; how exact they have to be, the bound alone decides.
No kernel may reach another device: no remote copies, remote signals or barrier semaphores. Data moves between devices by JAX's collectives and lax.ppermute only.
A program may use at most 128 MiB of HBM per device.

v0:
```python
import jax
import jax.numpy as jnp
from jax import lax
from jax.sharding import PartitionSpec as P

NB = 128
LB = 16
SB = 3


def swapped(value, axis, distance):
    mask = 2**distance
    pairs = [(source, source ^ mask) for source in range(lax.axis_size(axis))]
    return lax.ppermute(value, axis, pairs)


def apply_lower(matrix, vector):
    return jnp.dot(matrix, vector.astype(jnp.bfloat16), preferred_element_type=jnp.float32)


def apply_upper(matrix, vector):
    return jnp.dot(matrix.T, vector.astype(jnp.bfloat16), preferred_element_type=jnp.float32)


def right_lower(vector_rows, matrix):
    return jnp.dot(vector_rows.astype(jnp.bfloat16), matrix.T, preferred_element_type=jnp.float32)


def right_upper(vector_rows, matrix):
    return jnp.dot(vector_rows.astype(jnp.bfloat16), matrix, preferred_element_type=jnp.float32)


def block_lookup_tables(below, parents):
    targets = jnp.concatenate([parents, jnp.full((1,), LB, jnp.int32)])
    padded = jnp.concatenate([below, jnp.zeros((1, NB, NB), below.dtype)], axis=0)
    orders = jnp.arange(LB, dtype=jnp.int32)
    return (targets, padded, orders)


def local_forward(righthand, inverse, below, parents):
    columns = righthand.shape[1]
    blocks = righthand.reshape(LB, NB, columns)
    targets, padded, orders = block_lookup_tables(below, parents)

    def advance(carried, items):
        current, inv_block, low_block, target, number = items
        result = apply_lower(inv_block, current - carried[number])
        carried = carried.at[target].add(apply_lower(low_block, result))
        return (carried, result)

    start = jnp.zeros((LB + 1, NB, columns), jnp.float32)
    _, results = lax.scan(advance, start, (blocks, inverse, padded, targets, orders))
    return results.reshape(LB * NB, columns)


def local_backward(forward, update_terms, inverse, below, parents):
    columns = forward.shape[1]
    remains = (forward - update_terms).reshape(LB, NB, columns)
    targets, padded, orders = block_lookup_tables(below, parents)

    def retreat(carried, items):
        current, inv_block, low_block, target, number = items
        result = apply_upper(inv_block, current - apply_upper(low_block, carried[target]))
        carried = carried.at[number].set(result.astype(jnp.bfloat16))
        return (carried, result)

    start = jnp.zeros((LB + 1, NB, columns), jnp.bfloat16)
    _, results = lax.scan(retreat, start, (remains, inverse, padded, targets, orders), reverse=True)
    return results.reshape(LB * NB, columns)


def separator_forward(righthand, inverse, lowerpart):
    solved = []
    rounded = []
    for position in range(SB):
        current = righthand[:, position * NB : (position + 1) * NB]
        if position > 0:
            earlier = jnp.concatenate(rounded, axis=1)
            current = current - jnp.dot(
                earlier,
                lowerpart[position * NB : (position + 1) * NB, : position * NB].T,
                preferred_element_type=jnp.float32,
            )
        result = right_lower(current, inverse[position])
        solved.append(result)
        rounded.append(result.astype(jnp.bfloat16))
    return (jnp.concatenate(solved, axis=1), jnp.concatenate(rounded, axis=1))


def separator_backward(righthand, inverse, lowerpart):
    solved = [None] * SB
    rounded = [None] * SB
    for position in reversed(range(SB)):
        current = righthand[:, position * NB : (position + 1) * NB]
        if position < SB - 1:
            later = jnp.concatenate(rounded[position + 1 :], axis=1)
            current = current - right_upper(
                later, lowerpart[(position + 1) * NB :, position * NB : (position + 1) * NB]
            )
        result = right_upper(current, inverse[position])
        solved[position] = result
        rounded[position] = result.astype(jnp.bfloat16)
    return (jnp.concatenate(solved, axis=1), jnp.concatenate(rounded, axis=1))


def pick_entry(array, number):
    return lax.dynamic_index_in_dim(array, number, 0, keepdims=False)


def separator_chain(updates, separator_right, separator_inverse, separator_lower, parent_coupling):
    leaf_count = lax.axis_size("leaf")
    levels = leaf_count.bit_length() - 1
    leaf_index = lax.axis_index("leaf")
    remaining = updates
    forward_seps = []
    numbers = []
    inverse_blocks = []
    lowers = []
    for height in range(1, levels + 1):
        remaining = remaining + swapped(remaining, "leaf", height - 1)
        number = (leaf_count >> height) - 1 + (leaf_index >> height)
        right_rows = pick_entry(separator_right, number).T
        inverse = pick_entry(separator_inverse, number)
        lowerpart = pick_entry(separator_lower, number)
        result, result_round = separator_forward(right_rows - remaining[0], inverse, lowerpart)
        forward_seps.append(result)
        numbers.append(number)
        inverse_blocks.append(inverse)
        lowers.append(lowerpart)
        if height < levels:
            coupling_matrix = pick_entry(parent_coupling, number - 1)
            remaining = remaining[1:]
            remaining = remaining.at[0].add(
                jnp.dot(result_round, coupling_matrix.T, preferred_element_type=jnp.float32)
            )
    solutions = [None] * levels
    above_round = None
    for height in range(levels, 0, -1):
        upward = forward_seps[height - 1]
        if height < levels:
            coupling_matrix = pick_entry(parent_coupling, numbers[height - 1] - 1)
            upward = upward - right_upper(above_round, coupling_matrix)
        result, above_round = separator_backward(
            upward, inverse_blocks[height - 1], lowers[height - 1]
        )
        solutions[height - 1] = result
    return jnp.stack(solutions, axis=0)


def on_device(
    local_right,
    local_inverse,
    local_below,
    local_parent,
    local_coupling,
    separator_right,
    separator_inverse,
    separator_lower,
    parent_coupling,
):
    forward = local_forward(
        local_right[0, 0], local_inverse[0, 0], local_below[0, 0], local_parent[0, 0]
    )
    coupling_matrix = local_coupling[0, 0]
    forward_pass_rounded = forward.astype(jnp.bfloat16)
    partials = jnp.einsum(
        "ekx,xn->enk", coupling_matrix, forward_pass_rounded, preferred_element_type=jnp.float32
    )
    updates = lax.psum(partials, "rep")
    solved = separator_chain(
        updates, separator_right, separator_inverse, separator_lower, parent_coupling
    )
    rounded_solution_rows = solved.astype(jnp.bfloat16)
    update_terms = jnp.einsum(
        "apy,anp->yn", coupling_matrix, rounded_solution_rows, preferred_element_type=jnp.float32
    )
    local_solution = local_backward(
        forward, update_terms, local_inverse[0, 0], local_below[0, 0], local_parent[0, 0]
    )
    return (local_solution[None, None], jnp.swapaxes(solved, 1, 2)[None])


def solution(mesh):
    in_specs = (
        P("leaf", "rep", None, None),
        P("leaf", "rep", None, None, None),
        P("leaf", "rep", None, None, None),
        P("leaf", "rep", None),
        P("leaf", "rep", None, None, None),
        P(),
        P(),
        P(),
        P(),
    )
    out_specs = (P("leaf", "rep", None, None), P("leaf", None, None, None))
    return jax.shard_map(
        on_device, mesh=mesh, in_specs=in_specs, out_specs=out_specs, check_vma=False
    )
```

profile of v0, /device:TPU:0, one launch (start us, length us, event | category | flops | bytes accessed | tf_op | source)
XLA Modules:
  0.0 457.7 jit_solution(9730714361711297936)
XLA Ops:
  10.4 144.4 %while.33 = (s32[]{:T(128)}, f32[17,128,128]{2,1,0:T(8,128)}, f32[16,128,128]{2,1,0:T(8,128)S(1)}, s32[16]{0:T(128)S(1)}, bf16[16,128,128]{2,1,0:T(8,128)(2,1)S(...) while((s32[]{:T(128)}, f32[17,128,128]{2,1,0:T(8,128)}, ...), condition=%wide.region_2.3_spmd, body=%wide.region_0.2_spmd.sunk | while | flops 8470553 | bytes 462066 | solution.py:52
  17.2 2.2 fusion.409
  26.3 2.2 fusion.409
  35.3 2.2 fusion.409
  44.3 2.2 fusion.409
  53.4 2.2 fusion.409
  62.4 2.2 fusion.409
  71.4 2.2 fusion.409
  80.4 2.2 fusion.409
  89.5 2.2 fusion.409
  98.5 2.2 fusion.409
  107.5 2.2 fusion.409
  116.5 2.2 fusion.409
  125.5 2.2 fusion.409
  134.6 2.2 fusion.409
  143.6 2.2 fusion.409
  152.6 2.2 fusion.409
  154.9 6.0 %fusion.40 = f32[4,128,384]{2,1,0:T(8,128)} fusion(bf16[2048,128,1]{1,0,2:T(8,128)(2,1)S(1)} %bitcast.313, bf16[1,1,4,384,2048]{4,3,2,1,0:T(8,128)(2,1)} %param.27), kind=kOutput, calls=%fused_computation.38 | convolution fusion | flops 805306368 | bytes 7602176 | tf_op jit(solution)/shard_map/ekx,xn->enk/dot_general | solution.py:166
  161.0 78.8 %all-reduce.3.cloned.1.call-done = f32[4,128,384]{2,1,0:T(8,128)} async-done(((f32[4,128,384]{2,1,0:T(8,128)}), f32[4,128,384]{2,1,0:T(8,128)}) %all-reduce.3.cloned.1.call-update) | async-done | bytes 786448 | tf_op jit(solution)/shard_map/psum | solution.py:169
  239.8 2.0 constant_dynamic-slice_fusion.1
  242.6 2.4 dynamic-slice_bitcast_fusion
  250.4 1.9 fusion.332
  252.2 1.9 fusion.78
  256.5 13.8 %collective-permute-done.1 = f32[3,128,384]{2,1,0:T(8,128)} collective-permute-done((f32[3,128,384]{2,1,0:T(8,128)}, f32[3,128,384]{2,1,0:T(8,128)}, u32[]{:S(2)}, u32[]{:S(2)}) %collective-permute-start.1) | collective-permute-done | bytes 589856 | tf_op jit(solution)/shard_map/ppermute | solution.py:14
  274.9 1.9 fusion.341
  278.0 3.1 collective-permute-start.2
  282.8 7.6 %collective-permute-done.2 = f32[2,128,384]{2,1,0:T(8,128)} collective-permute-done((f32[2,128,384]{2,1,0:T(8,128)S(1)}, f32[2,128,384]{2,1,0:T(8,128)}, u32[]{:S(2)}, u32[]{:S(2)}) %collective-permute-start.2) | collective-permute-done | bytes 393248 | tf_op jit(solution)/shard_map/ppermute | solution.py:14
  296.7 1.9 slice_add_fusion
  298.6 2.7 collective-permute-start.3
  302.8 3.2 collective-permute-done.3
  321.9 3.8 fusion.37
  327.2 122.6 %while.34 = (s32[]{:T(128)}, bf16[17,128,128]{2,1,0:T(8,128)(2,1)S(1)}, f32[16,128,128]{2,1,0:T(8,128)S(1)}, s32[16]{0:T(128)S(1)}, bf16[16,128,128]{2,1,0:T(8,1...) while((s32[]{:T(128)}, ...), condition=%wide.region_6.7_spmd, body=%wide.region_4.6_spmd.sunk | while | flops 8454170 | bytes 363271 | solution.py:68
  (244 shorter events, 153.6 us)
Async XLA Ops:
  7.2 240.6 %copy-start = (bf16[15,3,128,128]{3,2,1,0:T(8,128)(2,1)S(1)}, bf16[15,3,128,128]{3,2,1,0:T(8,128)(2,1)}, u32[]{:S(2)}) copy-start(bf16[15,3,128,128]{3,2,1,0:T(8,128)(2,1)} %param.29) | copy-start | bytes 4423684
  7.2 232.6 %all-reduce.3.cloned.1.call-start = ((), (), s32[]{:S(2)}) async-start(), calls=%async_computation | async-start | bytes 1572864 | tf_op jit(solution)/shard_map/psum | solution.py:169
  7.2 3.2 copy-start.20
  154.8 6.1 %copy-start.2 = (bf16[16,128,128]{2,1,0:T(8,128)(2,1)}, bf16[16,128,128]{2,1,0:T(8,128)(2,1)S(1)}, u32[]{:S(2)}) copy-start(bf16[16,128,128]{2,1,0:T(8,128)(2,1)S(1)} %get-tuple-element.562) | copy-start | bytes 1572868
  239.8 5.2 %collective-permute-start = (f32[4,128,384]{2,1,0:T(8,128)}, f32[4,128,384]{2,1,0:T(8,128)}, u32[]{:S(2)}, u32[]{:S(2)}) collective-permute-start(f32[4,128,384]{2,1,0:T(8,128)} %all-reduce.3.cloned.1.call-done), channel_id=1, source_target_pairs={{0,8},{8,0},{16,24},{24,16},{32,40},{40,32},{48,56},{56,48},{64,72... | collective-permute-start | bytes 2359304 | tf_op jit(solution)/shard_map/ppermute | solution.py:14
  242.6 2.4 copy-start.10
  244.9 2.1 copy-start.6
  247.1 0.7 copy-start.8
  254.2 16.1 %collective-permute-start.1 = (f32[3,128,384]{2,1,0:T(8,128)}, f32[3,128,384]{2,1,0:T(8,128)}, u32[]{:S(2)}, u32[]{:S(2)}) collective-permute-start(f32[3,128,384]{2,1,0:T(8,128)} %fusion.78), channel_id=1, source_target_pairs={{0,16},{8,24},{16,0},{24,8},{32,48},{40,56},{48,32},{56,40},{64,80... | collective-permute-start | bytes 1769480 | tf_op jit(solution)/shard_map/ppermute | solution.py:14
  256.5 15.1 %copy-start.7 = (f32[1,384,128]{1,2,0:T(8,128)S(1)}, f32[1,384,128]{1,2,0:T(8,128)}, u32[]{:S(2)}) copy-start(f32[1,384,128]{1,2,0:T(8,128)} %copy.14) | copy-start | bytes 589828
  271.6 0.7 copy-start.9
  278.0 12.4 %collective-permute-start.2 = (f32[2,128,384]{2,1,0:T(8,128)S(1)}, f32[2,128,384]{2,1,0:T(8,128)}, u32[]{:S(2)}, u32[]{:S(2)}) collective-permute-start(f32[2,128,384]{2,1,0:T(8,128)S(1)} %fusion.76), channel_id=1, source_target_pairs={{0,32},{8,40},{16,48},{24,56},{32,0},{40,8},{48,16},{56,24},{64,96... | collective-permute-start | bytes 1179656 | tf_op jit(solution)/shard_map/ppermute | solution.py:14
  282.8 18.5 %copy-start.5 = (f32[1,384,128]{2,1,0:T(8,128)S(1)}, f32[1,384,128]{2,1,0:T(8,128)}, u32[]{:S(2)}) copy-start(f32[1,384,128]{2,1,0:T(8,128)} %get-tuple-element.317) | copy-start | bytes 589828
  298.6 7.4 %collective-permute-start.3 = (f32[1,128,384]{2,1,0:T(8,128)}, f32[1,128,384]{2,1,0:T(8,128)S(1)}, u32[]{:S(2)}, u32[]{:S(2)}) collective-permute-start(f32[1,128,384]{2,1,0:T(8,128)} %slice_add_fusion), channel_id=1, source_target_pairs={{0,64},{8,72},{16,80},{24,88},{32,96},{40,104},{48,112},{56,120},{... | collective-permute-start | bytes 589832 | tf_op jit(solution)/shard_map/ppermute | solution.py:14
  301.5 5.7 %copy-start.4 = (bf16[384,384]{1,0:T(8,128)(2,1)S(1)}, bf16[384,384]{1,0:T(8,128)(2,1)}, u32[]{:S(2)}) copy-start(bf16[384,384]{1,0:T(8,128)(2,1)} %get-tuple-element.310) | copy-start | bytes 884740
  302.8 6.0 %copy-start.15 = (f32[128,128]{0,1:T(8,128)S(1)}, f32[128,128]{0,1:T(8,128)}, u32[]{:S(2)}) copy-start(f32[128,128]{0,1:T(8,128)} %get-tuple-element.331) | copy-start | bytes 196612
  302.8 6.0 %copy-start.16 = (f32[128,128]{0,1:T(8,128)S(1)}, f32[128,128]{0,1:T(8,128)}, u32[]{:S(2)}) copy-start(f32[128,128]{0,1:T(8,128)} %get-tuple-element.335) | copy-start | bytes 196612
  302.8 6.0 %copy-start.19 = (f32[128,128]{0,1:T(8,128)S(1)}, f32[128,128]{0,1:T(8,128)}, u32[]{:S(2)}) copy-start(f32[128,128]{0,1:T(8,128)} %get-tuple-element.333) | copy-start | bytes 196612
  307.1 5.6 %copy-start.13 = (f32[128,128]{0,1:T(8,128)S(1)}, f32[128,128]{0,1:T(8,128)}, u32[]{:S(2)}) copy-start(f32[128,128]{0,1:T(8,128)} %get-tuple-element.325) | copy-start | bytes 196612
  307.1 5.6 %copy-start.14 = (f32[128,128]{0,1:T(8,128)S(1)}, f32[128,128]{0,1:T(8,128)}, u32[]{:S(2)}) copy-start(f32[128,128]{0,1:T(8,128)} %get-tuple-element.329) | copy-start | bytes 196612
  307.1 5.6 %copy-start.18 = (f32[128,128]{0,1:T(8,128)S(1)}, f32[128,128]{0,1:T(8,128)}, u32[]{:S(2)}) copy-start(f32[128,128]{0,1:T(8,128)} %get-tuple-element.327) | copy-start | bytes 196612
  308.8 7.8 %copy-start.11 = (f32[128,128]{0,1:T(8,128)S(1)}, f32[128,128]{0,1:T(8,128)}, u32[]{:S(2)}) copy-start(f32[128,128]{0,1:T(8,128)} %get-tuple-element.319) | copy-start | bytes 196612
  308.8 7.8 %copy-start.12 = (f32[128,128]{0,1:T(8,128)S(1)}, f32[128,128]{0,1:T(8,128)}, u32[]{:S(2)}) copy-start(f32[128,128]{0,1:T(8,128)} %get-tuple-element.323) | copy-start | bytes 196612
  308.8 7.8 %copy-start.17 = (f32[128,128]{0,1:T(8,128)S(1)}, f32[128,128]{0,1:T(8,128)}, u32[]{:S(2)}) copy-start(f32[128,128]{0,1:T(8,128)} %get-tuple-element.321) | copy-start | bytes 196612
  320.4 1.5 copy-start.1
  449.9 1.0 copy-start.3
Sparse Core Ops, SparseCore 0:
  161.1 78.6 all-reduce.2
where the time goes:
time: 463 us; the launch traced here: 458 us
  loops' own time  123 us (27%)
  matrix products  112 us (24%)
  waiting for transfers between devices  103 us (22%)
  local copies, waits for them, and re-layouts  55.8 us (12%)
  other arithmetic  41 us (9%)
  between operations  14.5 us (3%)
  starting transfers between devices  7.28 us (2%)
    psum x1, waiting for transfers between devices, on_device(): updates = lax.psum(partials, 'rep')  78.8 us
    another operation x1, loops' own time, local_forward(): lax.scan(advance, start, (blocks, inverse, padded, targets, orders))  62.2 us
    another operation x1, loops' own time, local_backward(): lax.scan(retreat, start, (remains, inverse, padded, targets, orders), rev...  61 us
    dot_general x32, matrix products, apply_lower(): jnp.dot(matrix, vector.astype(jnp.bfloat16), preferred_element_type=jnp.f...  51.9 us
    dynamic_slice x64, local copies, waits for them, and re-layouts, local_forward(): lax.scan(advance, start, (blocks, inverse, padded, targets, orders))  39 us
    ppermute x4, waiting for transfers between devices, swapped(): return lax.ppermute(value, axis, pairs)  24.6 us
    another operation x32, other arithmetic  23.2 us
    dot_general x16, matrix products, apply_upper(): jnp.dot(matrix.T, vector.astype(jnp.bfloat16), preferred_element_type=jnp...  19.2 us
  transfers between devices with their start and end apart: 5, of which 4 were waited for; matrix products, arithmetic and copies ran while one was open for 2% of the time, Pallas kernels for 0%

commit v1 on v0

--- a/solution.py
+++ b/solution.py
@@ -166,7 +166,7 @@
     partials = jnp.einsum(
         "ekx,xn->enk", coupling_matrix, forward_pass_rounded, preferred_element_type=jnp.float32
     )
-    updates = lax.psum(partials, "rep")
+    updates = jnp.sum(lax.all_gather(partials, "rep"), axis=0)
     solved = separator_chain(
         updates, separator_right, separator_inverse, separator_lower, parent_coupling
     )

time: 463 us -> 465 us (level)
    psum x1 -> x0, waiting for transfers between devices: 78.8 us -> none  [on_device(): updates = lax.psum(partials, 'rep')]
    all_gather x0 -> x1, waiting for transfers between devices: none -> 75.1 us  [on_device(): updates = jnp.sum(lax.all_gather(partials, 'rep'), axis=0)]
where the time goes in v1:
time: 465 us; the launch traced here: 459 us
  loops' own time  123 us (26%)
  matrix products  112 us (24%)
  waiting for transfers between devices  99.2 us (21%)
  local copies, waits for them, and re-layouts  56.9 us (12%)
  other arithmetic  45.5 us (10%)
  between operations  14.5 us (3%)
  starting transfers between devices  7.46 us (2%)
    all_gather x1, waiting for transfers between devices, on_device(): updates = jnp.sum(lax.all_gather(partials, 'rep'), axis=0)  75.1 us
    another operation x1, loops' own time, local_forward(): lax.scan(advance, start, (blocks, inverse, padded, targets, orders))  62.2 us
    another operation x1, loops' own time, local_backward(): lax.scan(retreat, start, (remains, inverse, padded, targets, orders), rev...  61 us
    dot_general x32, matrix products, apply_lower(): jnp.dot(matrix, vector.astype(jnp.bfloat16), preferred_element_type=jnp.f...  52.3 us
    dynamic_slice x64, local copies, waits for them, and re-layouts, local_forward(): lax.scan(advance, start, (blocks, inverse, padded, targets, orders))  39 us
    another operation x32, other arithmetic  24.2 us
    ppermute x4, waiting for transfers between devices, swapped(): return lax.ppermute(value, axis, pairs)  24.1 us
    dot_general x16, matrix products, apply_upper(): jnp.dot(matrix.T, vector.astype(jnp.bfloat16), preferred_element_type=jnp...  19.2 us
  transfers between devices with their start and end apart: 5, of which 4 were waited for; matrix products, arithmetic and copies ran while one was open for 2% of the time, Pallas kernels for 0%

profile of v1, /device:TPU:0, one launch (start us, length us, event | category | flops | bytes accessed | tf_op | source)
XLA Modules:
  0.0 459.1 jit_solution(243042955723787483)
XLA Ops:
  10.4 145.8 %while.33 = (s32[]{:T(128)}, f32[17,128,128]{2,1,0:T(8,128)}, f32[16,128,128]{2,1,0:T(8,128)S(1)}, s32[16]{0:T(128)S(1)}, bf16[16,128,128]{2,1,0:T(8,128)(2,1)S(...) while((s32[]{:T(128)}, f32[17,128,128]{2,1,0:T(8,128)}, ...), condition=%wide.region_2.3_spmd, body=%wide.region_0.2_spmd.sunk | while | flops 8470553 | bytes 462066 | solution.py:52
  17.3 2.2 fusion.409
  26.4 2.2 fusion.409
  35.5 2.2 fusion.409
  44.6 2.2 fusion.409
  53.7 2.2 fusion.409
  62.8 2.2 fusion.409
  71.9 2.2 fusion.409
  81.1 2.2 fusion.409
  90.2 2.2 fusion.409
  99.3 2.2 fusion.409
  108.4 2.2 fusion.409
  117.5 2.2 fusion.409
  126.6 2.2 fusion.409
  135.7 2.2 fusion.409
  144.9 2.2 fusion.409
  154.0 2.2 fusion.409
  156.3 6.0 %fusion.40 = f32[4,128,384]{2,1,0:T(8,128)} fusion(bf16[2048,128,1]{1,0,2:T(8,128)(2,1)S(1)} %bitcast.315, bf16[1,1,4,384,2048]{4,3,2,1,0:T(8,128)(2,1)} %param.27), kind=kOutput, calls=%fused_computation.38 | convolution fusion | flops 805306368 | bytes 7602176 | tf_op jit(solution)/shard_map/ekx,xn->enk/dot_general | solution.py:166
  162.4 75.1 %all-gather.3.cloned.1.call-done = f32[32,128,384]{2,1,0:T(8,128)} async-done(((f32[4,128,384]{2,1,0:T(8,128)}), f32[32,128,384]{2,1,0:T(8,128)}) %all-gather.3.cloned.1.call-update) | async-done | bytes 6291472 | tf_op jit(solution)/shard_map/all_gather | solution.py:169
  237.4 3.2 reduce_sum.9
  240.8 2.2 constant_dynamic-slice_fusion.1
  244.7 2.3 dynamic-slice_bitcast_fusion
  252.7 1.9 fusion.332
  254.6 1.9 fusion.78
  258.8 13.6 %collective-permute-done.1 = f32[3,128,384]{2,1,0:T(8,128)} collective-permute-done((f32[3,128,384]{2,1,0:T(8,128)}, f32[3,128,384]{2,1,0:T(8,128)}, u32[]{:S(2)}, u32[]{:S(2)}) %collective-permute-start.1) | collective-permute-done | bytes 589856 | tf_op jit(solution)/shard_map/ppermute | solution.py:14
  277.1 1.9 fusion.341
  280.2 3.1 collective-permute-start.2
  285.0 7.4 %collective-permute-done.2 = f32[2,128,384]{2,1,0:T(8,128)} collective-permute-done((f32[2,128,384]{2,1,0:T(8,128)S(1)}, f32[2,128,384]{2,1,0:T(8,128)}, u32[]{:S(2)}, u32[]{:S(2)}) %collective-permute-start.2) | collective-permute-done | bytes 393248 | tf_op jit(solution)/shard_map/ppermute | solution.py:14
  300.0 2.8 collective-permute-start.3
  304.3 3.1 collective-permute-done.3
  323.2 3.8 fusion.37
  328.6 122.6 %while.34 = (s32[]{:T(128)}, bf16[17,128,128]{2,1,0:T(8,128)(2,1)S(1)}, f32[16,128,128]{2,1,0:T(8,128)S(1)}, s32[16]{0:T(128)S(1)}, bf16[16,128,128]{2,1,0:T(8,1...) while((s32[]{:T(128)}, ...), condition=%wide.region_6.7_spmd, body=%wide.region_4.6_spmd.sunk | while | flops 8454170 | bytes 363271 | solution.py:68
  (247 shorter events, 157.2 us)
Async XLA Ops:
  7.2 242.9 %copy-start = (bf16[15,3,128,128]{3,2,1,0:T(8,128)(2,1)S(1)}, bf16[15,3,128,128]{3,2,1,0:T(8,128)(2,1)}, u32[]{:S(2)}) copy-start(bf16[15,3,128,128]{3,2,1,0:T(8,128)(2,1)} %param.29) | copy-start | bytes 4423684
  7.2 230.3 %all-gather.3.cloned.1.call-start = ((), (), s32[]{:S(2)}) async-start(), calls=%async_computation | async-start | bytes 7077888 | tf_op jit(solution)/shard_map/all_gather | solution.py:169
  7.2 3.2 copy-start.21
  156.2 6.1 %copy-start.3 = (bf16[16,128,128]{2,1,0:T(8,128)(2,1)}, bf16[16,128,128]{2,1,0:T(8,128)(2,1)S(1)}, u32[]{:S(2)}) copy-start(bf16[16,128,128]{2,1,0:T(8,128)(2,1)S(1)} %get-tuple-element.572) | copy-start | bytes 1572868
  240.6 6.4 %copy-start.2 = (f32[4,128,384]{2,1,0:T(8,128)}, f32[4,128,384]{2,1,0:T(8,128)S(1)}, u32[]{:S(2)}) copy-start(f32[4,128,384]{2,1,0:T(8,128)S(1)} %reduce_sum.9) | copy-start | bytes 2359300
  240.6 6.3 %collective-permute-start = (f32[4,128,384]{2,1,0:T(8,128)S(1)}, f32[4,128,384]{2,1,0:T(8,128)}, u32[]{:S(2)}, u32[]{:S(2)}) collective-permute-start(f32[4,128,384]{2,1,0:T(8,128)S(1)} %reduce_sum.9), channel_id=1, source_target_pairs={{0,8},{8,0},{16,24},{24,16},{32,40},{40,32},{48,56},{56,48},{64,72... | collective-permute-start | bytes 2359304 | tf_op jit(solution)/shard_map/ppermute | solution.py:14
  247.0 2.4 copy-start.7
  249.4 0.7 copy-start.9
  256.5 15.9 %collective-permute-start.1 = (f32[3,128,384]{2,1,0:T(8,128)}, f32[3,128,384]{2,1,0:T(8,128)}, u32[]{:S(2)}, u32[]{:S(2)}) collective-permute-start(f32[3,128,384]{2,1,0:T(8,128)} %fusion.78), channel_id=1, source_target_pairs={{0,16},{8,24},{16,0},{24,8},{32,48},{40,56},{48,32},{56,40},{64,80... | collective-permute-start | bytes 1769480 | tf_op jit(solution)/shard_map/ppermute | solution.py:14
  258.8 14.9 %copy-start.8 = (f32[1,384,128]{1,2,0:T(8,128)S(1)}, f32[1,384,128]{1,2,0:T(8,128)}, u32[]{:S(2)}) copy-start(f32[1,384,128]{1,2,0:T(8,128)} %copy.25) | copy-start | bytes 589828
  273.8 0.7 copy-start.10
  280.2 12.2 %collective-permute-start.2 = (f32[2,128,384]{2,1,0:T(8,128)S(1)}, f32[2,128,384]{2,1,0:T(8,128)}, u32[]{:S(2)}, u32[]{:S(2)}) collective-permute-start(f32[2,128,384]{2,1,0:T(8,128)S(1)} %fusion.76), channel_id=1, source_target_pairs={{0,32},{8,40},{16,48},{24,56},{32,0},{40,8},{48,16},{56,24},{64,96... | collective-permute-start | bytes 1179656 | tf_op jit(solution)/shard_map/ppermute | solution.py:14
  285.0 17.8 %copy-start.6 = (f32[1,384,128]{2,1,0:T(8,128)S(1)}, f32[1,384,128]{2,1,0:T(8,128)}, u32[]{:S(2)}) copy-start(f32[1,384,128]{2,1,0:T(8,128)} %get-tuple-element.325) | copy-start | bytes 589828
  296.9 1.8 copy-start.11
  300.0 7.4 %collective-permute-start.3 = (f32[1,128,384]{2,1,0:T(8,128)S(1)}, f32[1,128,384]{2,1,0:T(8,128)}, u32[]{:S(2)}, u32[]{:S(2)}) collective-permute-start(f32[1,128,384]{2,1,0:T(8,128)S(1)} %slice_add_fusion), channel_id=1, source_target_pairs={{0,64},{8,72},{16,80},{24,88},{32,96},{40,104},{48,112},{56,120},{... | collective-permute-start | bytes 589832 | tf_op jit(solution)/shard_map/ppermute | solution.py:14
  302.9 5.6 %copy-start.5 = (bf16[384,384]{1,0:T(8,128)(2,1)S(1)}, bf16[384,384]{1,0:T(8,128)(2,1)}, u32[]{:S(2)}) copy-start(bf16[384,384]{1,0:T(8,128)(2,1)} %get-tuple-element.318) | copy-start | bytes 884740
  304.3 5.8 %copy-start.16 = (f32[128,128]{0,1:T(8,128)S(1)}, f32[128,128]{0,1:T(8,128)}, u32[]{:S(2)}) copy-start(f32[128,128]{0,1:T(8,128)} %get-tuple-element.339) | copy-start | bytes 196612
  304.3 5.8 %copy-start.17 = (f32[128,128]{0,1:T(8,128)S(1)}, f32[128,128]{0,1:T(8,128)}, u32[]{:S(2)}) copy-start(f32[128,128]{0,1:T(8,128)} %get-tuple-element.343) | copy-start | bytes 196612
  304.3 5.9 %copy-start.20 = (f32[128,128]{0,1:T(8,128)S(1)}, f32[128,128]{0,1:T(8,128)}, u32[]{:S(2)}) copy-start(f32[128,128]{0,1:T(8,128)} %get-tuple-element.341) | copy-start | bytes 196612
  308.5 5.6 %copy-start.14 = (f32[128,128]{0,1:T(8,128)S(1)}, f32[128,128]{0,1:T(8,128)}, u32[]{:S(2)}) copy-start(f32[128,128]{0,1:T(8,128)} %get-tuple-element.333) | copy-start | bytes 196612
  308.5 5.6 %copy-start.15 = (f32[128,128]{0,1:T(8,128)S(1)}, f32[128,128]{0,1:T(8,128)}, u32[]{:S(2)}) copy-start(f32[128,128]{0,1:T(8,128)} %get-tuple-element.337) | copy-start | bytes 196612
  308.5 5.6 %copy-start.19 = (f32[128,128]{0,1:T(8,128)S(1)}, f32[128,128]{0,1:T(8,128)}, u32[]{:S(2)}) copy-start(f32[128,128]{0,1:T(8,128)} %get-tuple-element.335) | copy-start | bytes 196612
  310.1 7.8 %copy-start.12 = (f32[128,128]{0,1:T(8,128)S(1)}, f32[128,128]{0,1:T(8,128)}, u32[]{:S(2)}) copy-start(f32[128,128]{0,1:T(8,128)} %get-tuple-element.327) | copy-start | bytes 196612
  310.1 7.8 %copy-start.13 = (f32[128,128]{0,1:T(8,128)S(1)}, f32[128,128]{0,1:T(8,128)}, u32[]{:S(2)}) copy-start(f32[128,128]{0,1:T(8,128)} %get-tuple-element.331) | copy-start | bytes 196612
  310.1 7.8 %copy-start.18 = (f32[128,128]{0,1:T(8,128)S(1)}, f32[128,128]{0,1:T(8,128)}, u32[]{:S(2)}) copy-start(f32[128,128]{0,1:T(8,128)} %get-tuple-element.329) | copy-start | bytes 196612
  321.7 1.5 copy-start.1
  451.2 1.0 copy-start.4
Sparse Core Ops, SparseCore 0:
  162.5 74.9 all-gather.2
